TPU v7x, 32 devices: a whole 2x2x4 slice. The times are simulated.
32 devices in a mesh: groups: 2 (over y), seq: 4 (over z), adapt: 4 (over x, core).
Axes of the slice: x: 2, y: 2, z: 4, core: 2. Of those that a mesh axis runs over, the one named last changes fastest.
Arguments:
- image: bfloat16 [16, 2048, 3072], P(('groups', 'adapt'), 'seq'), parts along dimension 0, may hold values from -6 to 6
- modulation: float32 [16, 2, 3072], P(('groups', 'adapt')), parts along dimension 0, may hold values from -3 to 3
- query_key_value_weight: bfloat16 [3072, 6144], P(None, 'adapt'), may hold values from -0.109375 to 0.109375
- pooled_down_factor: bfloat16 [16, 3072, 64], P('seq'), may hold values from -0.109375 to 0.109375
- pooled_up_factor: bfloat16 [16, 64, 6144], P('seq', None, 'adapt'), may hold values from -0.75 to 0.75
- request_adapter: int32 [16], P('groups'), parts along dimension 0, may hold values from 0 to 15
- adapter_slot_table: int32 [16], replicated, may hold values from 0 to 15, each once
- row_request: int32 [16], P('groups'), parts along dimension 0, may hold values from 0 to 7, each once
- text_key_value: bfloat16 [16, 512, 2, 2048], P('groups', 'seq', None, 'adapt'), parts along dimension 0, may hold values from -110 to 110
- query_key_gain: float32 [2, 128], replicated, may hold values from 1 to 2.5
Outputs:
- attended: bfloat16 [16, 2048, 2048], P('groups', 'seq', 'adapt'), parts along dimension 0
There are 2 independent parts, one for each index of `groups`. A program takes and returns all parts, laid end to end along the dimension named above; an argument that names none is the same for every part. Nothing has to cross between parts.
All inputs are finite; a program needn't handle non-finite values.
Results may differ from a plain program's by a relative error of at most 0.0049.
The roundings to bfloat16 on the way count: a program that leaves them out, or rounds other values in their place, can miss the bound.
Values may be sent and summed in bfloat16 or wider, within the bound.
A program may use at most 192 MiB of HBM per device.

v0:
```python
import math
import jax
import jax.numpy as jnp
from jax import lax
from jax.sharding import PartitionSpec as P

HEAD_SIZE = 128


def layer_modulate(image, modulation):
    widened = image.astype(jnp.float32)
    centre = widened - jnp.mean(widened, axis=-1, keepdims=True)
    variance = jnp.mean(centre * centre, axis=-1, keepdims=True)
    normed = centre * lax.rsqrt(variance + 1e-06)
    return ((1.0 + modulation[:, 1, None, :]) * normed + modulation[:, 0, None, :]).astype(
        jnp.bfloat16
    )


def rms_scale(values, gain):
    return values * lax.rsqrt(jnp.mean(values * values, axis=-1, keepdims=True) + 1e-06) * gain


def attend_item(operands):
    queries, joined = operands
    key_rows = joined[:, 0]
    value_rows = joined[:, 1]
    query_count = queries.shape[0]
    block = math.gcd(query_count, 512)
    inverse = 1.0 / math.sqrt(queries.shape[-1])
    blocked = queries.reshape(query_count // block, block, queries.shape[-1])

    def one_block(block_rows):
        scores = (
            lax.dot_general(
                block_rows, key_rows, (((1,), (1,)), ((), ())), preferred_element_type=jnp.float32
            )
            * inverse
        )
        highest = jnp.max(scores, axis=-1, keepdims=True)
        weights = jnp.exp(scores - highest)
        weights = weights / jnp.sum(weights, axis=-1, keepdims=True)
        return jnp.dot(
            weights.astype(jnp.bfloat16), value_rows, preferred_element_type=jnp.float32
        ).astype(jnp.bfloat16)

    return lax.map(one_block, blocked).reshape(queries.shape)


def on_device(
    image,
    modulation,
    query_key_value_weight,
    pooled_down_factor,
    pooled_up_factor,
    request_adapter,
    adapter_slot_table,
    row_request,
    text_key_value,
    query_key_gain,
):
    seq_index = lax.axis_index("seq")
    all_requests = request_adapter.shape[0]
    local_pool_slice = pooled_down_factor.shape[0]
    pool_total = adapter_slot_table.shape[0]
    heads_local = query_key_value_weight.shape[1] // (3 * HEAD_SIZE)
    text_local = text_key_value.shape[1]
    modulated = layer_modulate(image, modulation)
    request_match = row_request[:, None] == jnp.arange(all_requests, dtype=jnp.int32)[None, :]
    chosen_ids = jnp.sum(jnp.where(request_match, request_adapter[None, :], 0), axis=1)
    slot_match = chosen_ids[:, None] == jnp.arange(pool_total, dtype=jnp.int32)[None, :]
    slots = jnp.sum(jnp.where(slot_match, adapter_slot_table[None, :], 0), axis=1)
    owned = slots // local_pool_slice == seq_index
    local_match = (slots % local_pool_slice)[:, None] == jnp.arange(
        local_pool_slice, dtype=jnp.int32
    )[None, :]
    slot_picker = (owned[:, None] & local_match).astype(jnp.bfloat16)
    up_terms = jnp.einsum(
        "eq,qfx->efx", slot_picker, pooled_up_factor, preferred_element_type=jnp.float32
    ).astype(jnp.bfloat16)
    down_terms = jnp.einsum(
        "mv,vna->mna", slot_picker, pooled_down_factor, preferred_element_type=jnp.float32
    ).astype(jnp.bfloat16)
    down_fetched, up_fetched = (
        lax.psum(down_terms, "seq").astype(jnp.float32),
        lax.psum(up_terms, "seq").astype(jnp.float32),
    )
    down_fetched = down_fetched.astype(jnp.bfloat16)
    up_fetched = up_fetched.astype(jnp.bfloat16)
    block_rows = lax.all_gather(modulated, "adapt", axis=0, tiled=True)
    shrunk = jnp.einsum(
        "rtd,rdk->rtk", block_rows, down_fetched, preferred_element_type=jnp.float32
    ).astype(jnp.bfloat16)
    frozen = jnp.einsum(
        "rtd,dc->rtc", block_rows, query_key_value_weight, preferred_element_type=jnp.float32
    )
    qkv = frozen + jnp.einsum(
        "rtk,rkc->rtc", shrunk, up_fetched, preferred_element_type=jnp.float32
    )
    token_local = qkv.shape[1]
    qkv = qkv.reshape(all_requests, token_local, heads_local, 3, HEAD_SIZE)
    queries = rms_scale(qkv[:, :, :, 0], query_key_gain[0]).astype(jnp.bfloat16)
    image_keys = rms_scale(qkv[:, :, :, 1], query_key_gain[1]).astype(jnp.bfloat16)
    image_values = qkv[:, :, :, 2].astype(jnp.bfloat16)
    image_pairs = jnp.transpose(jnp.stack([image_keys, image_values], axis=3), (0, 2, 1, 3, 4))
    text_pairs = jnp.transpose(
        text_key_value.reshape(all_requests, text_local, 2, heads_local, HEAD_SIZE), (0, 3, 1, 2, 4)
    )
    joined = jnp.concatenate([image_pairs, text_pairs], axis=2)
    joined = joined.reshape(all_requests * heads_local, token_local + text_local, 2, HEAD_SIZE)
    queries = jnp.transpose(queries, (0, 2, 1, 3)).reshape(
        all_requests * heads_local, token_local, HEAD_SIZE
    )
    query_items, joined_items = (
        lax.all_to_all(queries, "seq", split_axis=0, concat_axis=1, tiled=True),
        lax.all_to_all(joined, "seq", split_axis=0, concat_axis=1, tiled=True),
    )
    attended = lax.map(attend_item, (query_items, joined_items))
    returned = lax.all_to_all(attended, "seq", split_axis=1, concat_axis=0, tiled=True)
    returned = returned.reshape(all_requests, heads_local, token_local, HEAD_SIZE)
    return jnp.transpose(returned, (0, 2, 1, 3)).reshape(
        all_requests, token_local, heads_local * HEAD_SIZE
    )


def solution(mesh):
    in_specs = (
        P(("groups", "adapt"), "seq", None),
        P(("groups", "adapt"), None, None),
        P(None, "adapt"),
        P("seq", None, None),
        P("seq", None, "adapt"),
        P("groups"),
        P(),
        P("groups"),
        P("groups", "seq", None, "adapt"),
        P(),
    )
    out_specs = P("groups", "seq", "adapt")
    return jax.shard_map(
        on_device, mesh=mesh, in_specs=in_specs, out_specs=out_specs, check_vma=False
    )
```

profile of v0, /device:TPU:0, one launch (start us, length us, event | category | flops | bytes accessed | tf_op | source)
XLA Modules:
  0.0 888.3 jit_solution(3175267230559958143)
XLA Ops:
  9.2 2.8 convolution_convert_fusion
  12.1 3.1 convolution_convert_fusion.1
  15.2 3.7 convert_reduce_fusion
  18.9 4.5 fusion.10
  23.6 9.4 %fusion.13 = bf16[2,512,3072]{2,1,0:T(8,128)(2,1)} fusion(bf16[2,512,3072]{2,1,0:T(8,128)(2,1)} %param.14, f32[2,3072]{1,0:T(2,128)S(1)} %get-tuple-element.83, f32[2,512]{1,0:T(2,128)S(1)} %add_rsqrt_fusion.2, f32[2,512]{1,0:T(2,128)S(1)} %broadcast_multiply_fusion, f32[2,3072]{1,0:T(2,128)S(1)} %get-tuple-element.84), kind=kLoop, calls=%fused_computation.24 | loop fusion | flops 18874368 | bytes 12640256 | tf_op jit(solution)/shard_map/convert_element_type | solution.py:15
  34.2 156.1 %all-reduce.3.cloned.1.call-done = (bf16[8,64,1536]{2,0,1:T(8,128)(2,1)}, bf16[8,3072,64]{1,0,2:T(8,128)(2,1)}) async-done(((bf16[8,64,1536]{2,0,1:T(8,128)(2,1)}, bf16[8,3072,64]{1,0,2:T(8,128)(2,1)}), (bf16[8,64,1536]{2,0,1:T(8,128)(2,1)}, bf16[8,3072,64]{1,0,2:T(8,128)(2,1)})) %all-reduce.3.cloned.1.call-update) | async-done | bytes 4718608 | tf_op jit(solution)/shard_map/psum | solution.py:86
  190.3 23.9 %fusion.18 = f32[8,512,1536]{2,1,0:T(8,128)} fusion(bf16[8,64,1536]{2,0,1:T(8,128)(2,1)} %get-tuple-element.73, bf16[8,512,3072]{2,1,0:T(8,128)(2,1)} %all-gather.2.cloned.1.call-done, bf16[8,3072,64]{1,0,2:T(8,128)(2,1)} %get-tuple-element.74), kind=kOutput, calls=%fused_computation.40 | convolution fusion | flops 2416181248 | bytes 55050240 | tf_op jit(solution)/shard_map/rtk,rkc->rtc/dot_general | solution.py:97
  214.3 47.6 %convolution_add_fusion = f32[8,512,1536]{2,1,0:T(8,128)} fusion(f32[8,512,1536]{2,1,0:T(8,128)} %fusion.18, bf16[8,512,3072]{2,1,0:T(8,128)(2,1)} %all-gather.2.cloned.1.call-done, bf16[3072,1536]{1,0:T(8,128)(2,1)} %param.16), kind=kOutput, calls=%fused_computation.16 | convolution fusion | flops 38660997120 | bytes 84934656 | tf_op jit(solution)/shard_map/rtd,dc->rtc/dot_general | solution.py:94
  261.9 24.7 %copy.49 = f32[8,512,1536]{1,2,0:T(8,128)} copy(f32[8,512,1536]{2,1,0:T(8,128)} %convolution_add_fusion) | data formatting | bytes 50331648 | tf_op jit(solution)/shard_map/add | solution.py:97
  286.6 4.6 multiply_reduce_fusion.1
  291.2 7.0 fusion.15
  298.2 6.5 copy.50
  304.6 5.2 all-to-all-start
  309.8 6.2 copy.52
  316.0 3.2 copy.79
  319.1 4.0 slice.55
  323.1 4.6 multiply_reduce_fusion
  327.8 7.0 multiply_convert_fusion
  334.7 6.2 maximum_bitcast_fusion
  340.9 9.1 %pad_maximum_fusion = bf16[8,4,640,2,128]{2,4,3,1,0:T(8,128)(2,1)} fusion(bf16[8,4,128,2,128]{2,4,3,1,0:T(8,128)(2,1)} %bitcast.102, bf16[8,4,512,2,128]{2,4,3,1,0:T(8,128)(2,1)} %maximum_bitcast_fusion), kind=kLoop, calls=%fused_computation.25 | loop fusion | flops 20971520 | bytes 20971520 | tf_op jit(solution)/shard_map/concatenate | solution.py:109
  350.1 15.1 %copy.54 = bf16[8,4,640,2,128]{4,2,3,1,0:T(8,128)(2,1)} copy(bf16[8,4,640,2,128]{2,4,3,1,0:T(8,128)(2,1)} %pad_maximum_fusion) | data formatting | bytes 20971520 | tf_op jit(solution)/shard_map/concatenate | solution.py:109
  365.2 38.2 %all-to-all-done = bf16[32,512,128]{2,1,0:T(8,128)(2,1)} async-done(((bf16[32,512,128]{2,1,0:T(8,128)(2,1)}), bf16[32,512,128]{2,1,0:T(8,128)(2,1)}, u32[]{:S(2)}, u32[]{:S(2)}) %all-to-all-start) | async-done | bytes 4194336 | tf_op jit(solution)/shard_map/all_to_all | solution.py:115
  403.3 6.0 all-to-all-start.1
  409.4 4.6 copy.51
  414.0 223.2 %all-to-all-done.1 = bf16[32,640,2,128]{3,1,2,0:T(8,128)(2,1)} async-done(((bf16[32,640,2,128]{3,1,2,0:T(8,128)(2,1)}), bf16[32,640,2,128]{3,1,2,0:T(8,128)(2,1)}, u32[]{:S(2)}, u32[]{:S(2)}) %all-to-all-start.1) | async-done | bytes 10485792 | tf_op jit(solution)/shard_map/all_to_all | solution.py:116
  637.1 9.2 %copy.55 = bf16[8,4,640,2,128]{4,2,1,3,0:T(8,128)(2,1)} copy(bf16[8,4,640,2,128]{4,2,3,0,1:T(8,128)(2,1)} %bitcast.23) | data formatting | bytes 20971520 | tf_op jit(solution)/shard_map/all_to_all | solution.py:116
  646.3 118.3 %while.21 = (s32[]{:T(128)}, bf16[8,2048,128]{2,1,0:T(8,128)(2,1)}, bf16[8,2048,128]{2,1,0:T(8,128)(2,1)}, bf16[8,2560,2,128]{3,1,2,0:T(8,128)(2,1)}, s32[]{:T(128)}, /*index=5*/s32[]{:T(128)}, s32[]{:T(128)}) while((s32[]{:T(128)}, bf16[8,2048,128]{2,1,0:T(8,128)(2,1)}, bf16[8,2048,128]{2,1,0:T(8,128)(2,1)}, ...), condition=%wide.region_13.14_spmd, body=%wide.region_8.13_spmd.sunk | while | flops 680328192 | bytes 24652504 | solution.py:118
  646.3 1.4 dynamic-slice_bitcast_fusion.2
  648.9 11.3 %while.22 = (s32[]{:T(128)}, bf16[4,512,128]{2,1,0:T(8,128)(2,1)S(1)}, bf16[4,512,128]{2,1,0:T(8,128)(2,1)S(1)}, bf16[2560,128]{1,0:T(8,128)(2,1)S(1)}, bf16[2560,128]{1,0:T(8,128)(2,1)S(1)}, /*index=5*/s32[]{:T(128)}) while((s32[]{:T(128)}, bf16[4,512,128]{2,1,0:T(8,128)(2,1)S(1)}, bf16[4,512,128]{2,1,0:T(8,128)(2,1)S(1)}, ...), condition=%wide.region_12.12_spmd, body=%wide.region_9.11_spmd.sunk | while | flops 680328192 | bytes 17311820 | solution.py:47
  661.1 1.4 dynamic-slice_bitcast_fusion.2
  663.7 11.4 %while.22 = (s32[]{:T(128)}, bf16[4,512,128]{2,1,0:T(8,128)(2,1)S(1)}, bf16[4,512,128]{2,1,0:T(8,128)(2,1)S(1)}, bf16[2560,128]{1,0:T(8,128)(2,1)S(1)}, bf16[2560,128]{1,0:T(8,128)(2,1)S(1)}, /*index=5*/s32[]{:T(128)}) while((s32[]{:T(128)}, bf16[4,512,128]{2,1,0:T(8,128)(2,1)S(1)}, bf16[4,512,128]{2,1,0:T(8,128)(2,1)S(1)}, ...), condition=%wide.region_12.12_spmd, body=%wide.region_9.11_spmd.sunk | while | flops 680328192 | bytes 17311820 | solution.py:47
  675.9 1.4 dynamic-slice_bitcast_fusion.2
  678.5 11.4 %while.22 = (s32[]{:T(128)}, bf16[4,512,128]{2,1,0:T(8,128)(2,1)S(1)}, bf16[4,512,128]{2,1,0:T(8,128)(2,1)S(1)}, bf16[2560,128]{1,0:T(8,128)(2,1)S(1)}, bf16[2560,128]{1,0:T(8,128)(2,1)S(1)}, /*index=5*/s32[]{:T(128)}) while((s32[]{:T(128)}, bf16[4,512,128]{2,1,0:T(8,128)(2,1)S(1)}, bf16[4,512,128]{2,1,0:T(8,128)(2,1)S(1)}, ...), condition=%wide.region_12.12_spmd, body=%wide.region_9.11_spmd.sunk | while | flops 680328192 | bytes 17311820 | solution.py:47
  690.7 1.4 dynamic-slice_bitcast_fusion.2
  693.3 11.4 %while.22 = (s32[]{:T(128)}, bf16[4,512,128]{2,1,0:T(8,128)(2,1)S(1)}, bf16[4,512,128]{2,1,0:T(8,128)(2,1)S(1)}, bf16[2560,128]{1,0:T(8,128)(2,1)S(1)}, bf16[2560,128]{1,0:T(8,128)(2,1)S(1)}, /*index=5*/s32[]{:T(128)}) while((s32[]{:T(128)}, bf16[4,512,128]{2,1,0:T(8,128)(2,1)S(1)}, bf16[4,512,128]{2,1,0:T(8,128)(2,1)S(1)}, ...), condition=%wide.region_12.12_spmd, body=%wide.region_9.11_spmd.sunk | while | flops 680328192 | bytes 17311820 | solution.py:47
  705.5 1.4 dynamic-slice_bitcast_fusion.2
  708.1 11.4 %while.22 = (s32[]{:T(128)}, bf16[4,512,128]{2,1,0:T(8,128)(2,1)S(1)}, bf16[4,512,128]{2,1,0:T(8,128)(2,1)S(1)}, bf16[2560,128]{1,0:T(8,128)(2,1)S(1)}, bf16[2560,128]{1,0:T(8,128)(2,1)S(1)}, /*index=5*/s32[]{:T(128)}) while((s32[]{:T(128)}, bf16[4,512,128]{2,1,0:T(8,128)(2,1)S(1)}, bf16[4,512,128]{2,1,0:T(8,128)(2,1)S(1)}, ...), condition=%wide.region_12.12_spmd, body=%wide.region_9.11_spmd.sunk | while | flops 680328192 | bytes 17311820 | solution.py:47
  720.3 1.4 dynamic-slice_bitcast_fusion.2
  722.9 11.4 %while.22 = (s32[]{:T(128)}, bf16[4,512,128]{2,1,0:T(8,128)(2,1)S(1)}, bf16[4,512,128]{2,1,0:T(8,128)(2,1)S(1)}, bf16[2560,128]{1,0:T(8,128)(2,1)S(1)}, bf16[2560,128]{1,0:T(8,128)(2,1)S(1)}, /*index=5*/s32[]{:T(128)}) while((s32[]{:T(128)}, bf16[4,512,128]{2,1,0:T(8,128)(2,1)S(1)}, bf16[4,512,128]{2,1,0:T(8,128)(2,1)S(1)}, ...), condition=%wide.region_12.12_spmd, body=%wide.region_9.11_spmd.sunk | while | flops 680328192 | bytes 17311820 | solution.py:47
  735.1 1.4 dynamic-slice_bitcast_fusion.2
  737.6 11.4 %while.22 = (s32[]{:T(128)}, bf16[4,512,128]{2,1,0:T(8,128)(2,1)S(1)}, bf16[4,512,128]{2,1,0:T(8,128)(2,1)S(1)}, bf16[2560,128]{1,0:T(8,128)(2,1)S(1)}, bf16[2560,128]{1,0:T(8,128)(2,1)S(1)}, /*index=5*/s32[]{:T(128)}) while((s32[]{:T(128)}, bf16[4,512,128]{2,1,0:T(8,128)(2,1)S(1)}, bf16[4,512,128]{2,1,0:T(8,128)(2,1)S(1)}, ...), condition=%wide.region_12.12_spmd, body=%wide.region_9.11_spmd.sunk | while | flops 680328192 | bytes 17311820 | solution.py:47
  749.8 1.4 dynamic-slice_bitcast_fusion.2
  752.4 11.4 %while.22 = (s32[]{:T(128)}, bf16[4,512,128]{2,1,0:T(8,128)(2,1)S(1)}, bf16[4,512,128]{2,1,0:T(8,128)(2,1)S(1)}, bf16[2560,128]{1,0:T(8,128)(2,1)S(1)}, bf16[2560,128]{1,0:T(8,128)(2,1)S(1)}, /*index=5*/s32[]{:T(128)}) while((s32[]{:T(128)}, bf16[4,512,128]{2,1,0:T(8,128)(2,1)S(1)}, bf16[4,512,128]{2,1,0:T(8,128)(2,1)S(1)}, ...), condition=%wide.region_12.12_spmd, body=%wide.region_9.11_spmd.sunk | while | flops 680328192 | bytes 17311820 | solution.py:47
  764.6 4.9 copy.56
  769.5 95.4 %all_to_all.51 = bf16[8,2048,128]{2,0,1:T(8,128)(2,1)S(1)} all-to-all(bf16[8,2048,128]{2,0,1:T(8,128)(2,1)S(1)} %copy.56), channel_id=1, replica_groups=mesh['groups'=2,'seq'=4,'adapt'=4] {'seq'}, dimensions={1} | all-to-all | bytes 8388608 | tf_op jit(solution)/shard_map/all_to_all | solution.py:119
  864.9 2.9 copy.58
  867.8 6.6 copy.59
  874.4 6.4 copy.60
  (155 shorter events, 109.5 us)
Async XLA Ops:
  7.4 1.8 copy-start
  7.4 182.9 %all-reduce.3.cloned.1.call-start = ((), (), s32[]{:S(2)}) async-start(), calls=%async_computation.4 | async-start | bytes 9437184 | tf_op jit(solution)/shard_map/psum | solution.py:86
  15.2 8.3 copy-start.2
  15.2 175.1 %all-gather.2.cloned.1.call-start = ((), (), s32[]{:S(2)}) async-start(), calls=%async_computation.3 | async-start | bytes 31457280 | tf_op jit(solution)/shard_map/all_gather | solution.py:90
  33.0 0.7 copy-start.4
  304.6 98.7 %all-to-all-start = ((bf16[32,512,128]{2,1,0:T(8,128)(2,1)}), bf16[32,512,128]{2,1,0:T(8,128)(2,1)}, u32[]{:S(2)}, u32[]{:S(2)}) async-start(bf16[32,512,128]{2,1,0:T(8,128)(2,1)} %bitcast.96), calls=%async_computation | async-start | bytes 8388608 | tf_op jit(solution)/shard_map/all_to_all | solution.py:115
  323.1 4.6 copy-start.3
  403.3 233.8 %all-to-all-start.1 = ((bf16[32,640,2,128]{3,1,2,0:T(8,128)(2,1)}), bf16[32,640,2,128]{3,1,2,0:T(8,128)(2,1)}, u32[]{:S(2)}, u32[]{:S(2)}) async-start(bf16[32,640,2,128]{3,1,2,0:T(8,128)(2,1)} %bitcast.94), calls=%async_computation.1 | async-start | bytes 20971520 | tf_op jit(solution)/shard_map/all_to_all | solution.py:116
  867.8 13.0 %copy-start.1 = (bf16[4,3072,64]{1,2,0:T(8,128)(2,1)S(1)}, bf16[4,3072,64]{1,2,0:T(8,128)(2,1)}, u32[]{:S(2)}) copy-start(bf16[4,3072,64]{1,2,0:T(8,128)(2,1)} %param.17) | copy-start | bytes 4718596
Sparse Core Ops, SparseCore 0:
  15.3 174.9 all-reduce.2
Sparse Core Ops, SparseCore 1:
  33.1 157.0 all-gather.1
where the time goes:
time: 891 us; the launch traced here: 888 us
  waiting for transfers between devices  417 us (47%)
  matrix products  141 us (16%)
  local copies, waits for them, and re-layouts  123 us (14%)
  blocking collectives  95.4 us (11%)
  other arithmetic  85 us (10%)
  between operations  15 us (2%)
  starting transfers between devices  11.2 us (1%)
    all_to_all x1, waiting for transfers between devices, on_device(): lax.all_to_all(joined, 'seq', split_axis=0, concat_axis=1, tiled=True)  223 us
    psum x1, waiting for transfers between devices, on_device(): lax.psum(up_terms, 'seq').astype(jnp.float32)  156 us
    all_to_all x1, blocking collectives, on_device(): lax.all_to_all(attended, 'seq', split_axis=1, concat_axis=0, tiled=True)  95.4 us
    dot_general x1, matrix products, on_device(): jnp.einsum('rtd,dc->rtc', block_rows, query_key_value_weight, preferred_e...  47.6 us
    all_to_all x1, waiting for transfers between devices, on_device(): lax.all_to_all(queries, 'seq', split_axis=0, concat_axis=1, tiled=True)  38.2 us
    dot_general x32, matrix products, one_block(): jnp.dot(weights.astype(jnp.bfloat16), value_rows, preferred_element_type=...  33.5 us
    dot_general x32, matrix products, one_block(): lax.dot_general(block_rows, key_rows, (((1,), (1,)), ((), ())), preferred...  29.7 us
    reduce_sum x32, other arithmetic, one_block(): weights = weights / jnp.sum(weights, axis=-1, keepdims=True)  27 us
  transfers between devices with their start and end apart: 4, of which 3 were waited for; matrix products, arithmetic and copies ran while one was open for 9% of the time, Pallas kernels for 0%

commit v1 on v0

--- a/solution.py
+++ b/solution.py
@@ -83,7 +83,7 @@
     ).astype(jnp.bfloat16)
     down_fetched, up_fetched = (
         lax.psum(down_terms, "seq").astype(jnp.float32),
-        lax.psum(up_terms, "seq").astype(jnp.float32),
+        jnp.sum(lax.all_gather(up_terms, "seq"), axis=0).astype(jnp.float32),
     )
     down_fetched = down_fetched.astype(jnp.bfloat16)
     up_fetched = up_fetched.astype(jnp.bfloat16)

time: 891 us -> 1100 us (1.23)
  waiting for transfers between devices: 417 us -> 631 us
    all_gather x1, waiting for transfers between devices: 0.01 us -> 155 us  [on_device(): block_rows = lax.all_gather(modulated, 'adapt', axis=0, tiled=True)]
    all_gather x0 -> x1, waiting for transfers between devices: none -> 96 us  [on_device(): lax.all_gather(up_terms, 'seq')]
    psum x1, waiting for transfers between devices: 156 us -> 117 us  [on_device(): lax.psum(down_terms, 'seq').astype(jnp.float32)]
  transfers between devices with their start and end apart: 4 -> 5, of which waited for: 3 -> 5; matrix products, arithmetic and copies ran while one was open for 9% -> 8% of each run, Pallas kernels for 0% -> 0%
where the time goes in v1:
time: 1100 us
  waiting for transfers between devices  631 us (57%)
  matrix products  139 us (13%)
  local copies, waits for them, and re-layouts  123 us (11%)
  blocking collectives  95.2 us (9%)
  other arithmetic  89.5 us (8%)
  between operations  13.3 us (1%)
  starting transfers between devices  11.2 us (1%)
    all_to_all x1, waiting for transfers between devices, on_device(): lax.all_to_all(joined, 'seq', split_axis=0, concat_axis=1, tiled=True)  223 us
    all_gather x1, waiting for transfers between devices, on_device(): block_rows = lax.all_gather(modulated, 'adapt', axis=0, tiled=True)  155 us
    psum x1, waiting for transfers between devices, on_device(): lax.psum(down_terms, 'seq').astype(jnp.float32)  117 us
    all_gather x1, waiting for transfers between devices, on_device(): lax.all_gather(up_terms, 'seq')  96 us
    all_to_all x1, blocking collectives, on_device(): lax.all_to_all(attended, 'seq', split_axis=1, concat_axis=0, tiled=True)  95.2 us
    dot_general x1, matrix products, on_device(): jnp.einsum('rtd,dc->rtc', block_rows, query_key_value_weight, preferred_e...  47.6 us
    all_to_all x1, waiting for transfers between devices, on_device(): lax.all_to_all(queries, 'seq', split_axis=0, concat_axis=1, tiled=True)  38.3 us
    dot_general x32, matrix products, one_block(): jnp.dot(weights.astype(jnp.bfloat16), value_rows, preferred_element_type=...  33.5 us
  transfers between devices with their start and end apart: 5, of which 5 were waited for; matrix products, arithmetic and copies ran while one was open for 8% of the time, Pallas kernels for 0%

profile of v1, /device:TPU:0, one launch (start us, length us, event | category | flops | bytes accessed | tf_op | source)
XLA Modules:
  0.0 1102.3 jit_solution(8052979319058100334)
XLA Ops:
  8.4 3.1 convolution_convert_fusion.1
  11.5 2.8 convolution_convert_fusion
  14.5 3.7 convert_reduce_fusion
  18.1 4.7 fusion.10
  22.9 9.6 fusion.13
  33.7 96.0 %all-gather.6.cloned.1.call-done = bf16[32,64,1536]{2,0,1:T(8,128)(2,1)} async-done(((bf16[8,64,1536]{2,0,1:T(8,128)(2,1)}), bf16[32,64,1536]{2,0,1:T(8,128)(2,1)}) %all-gather.6.cloned.1.call-update) | async-done | bytes 6291472 | tf_op jit(solution)/shard_map/all_gather | solution.py:86
  129.7 4.2 bitcast_reduce_fusion
  133.9 117.5 %all-reduce.2.cloned.1.call-done = bf16[8,3072,64]{1,0,2:T(8,128)(2,1)} async-done(((bf16[8,3072,64]{1,0,2:T(8,128)(2,1)}), bf16[8,3072,64]{1,0,2:T(8,128)(2,1)}) %all-reduce.2.cloned.1.call-update) | async-done | bytes 3145744 | tf_op jit(solution)/shard_map/psum | solution.py:85
  251.3 155.4 %all-gather.4.cloned.1.call-done = bf16[8,512,3072]{2,1,0:T(8,128)(2,1)} async-done(((bf16[2,512,3072]{2,1,0:T(8,128)(2,1)}), bf16[8,512,3072]{2,1,0:T(8,128)(2,1)}) %all-gather.4.cloned.1.call-update) | async-done | bytes 25165840 | tf_op jit(solution)/shard_map/all_gather | solution.py:90
  406.8 22.3 %fusion.18 = f32[8,512,1536]{2,1,0:T(8,128)} fusion(bf16[8,64,1536]{2,0,1:T(8,128)(2,1)S(1)} %bitcast_reduce_fusion, bf16[8,512,3072]{2,1,0:T(8,128)(2,1)} %all-gather.4.cloned.1.call-done, bf16[8,3072,64]{1,0,2:T(8,128)(2,1)} %all-reduce.2.cloned.1.call-done), kind=kOutput, calls=%fused_computation.41 | convolution fusion | flops 2416181248 | bytes 55050240 | tf_op jit(solution)/shard_map/rtk,rkc->rtc/dot_general | solution.py:97
  429.1 47.6 %convolution_add_fusion = f32[8,512,1536]{2,1,0:T(8,128)} fusion(f32[8,512,1536]{2,1,0:T(8,128)} %fusion.18, bf16[8,512,3072]{2,1,0:T(8,128)(2,1)} %all-gather.4.cloned.1.call-done, bf16[3072,1536]{1,0:T(8,128)(2,1)} %param.16), kind=kOutput, calls=%fused_computation.16 | convolution fusion | flops 38660997120 | bytes 84934656 | tf_op jit(solution)/shard_map/rtd,dc->rtc/dot_general | solution.py:94
  476.7 24.7 %copy.50 = f32[8,512,1536]{1,2,0:T(8,128)} copy(f32[8,512,1536]{2,1,0:T(8,128)} %convolution_add_fusion) | data formatting | bytes 50331648 | tf_op jit(solution)/shard_map/add | solution.py:97
  501.4 4.6 multiply_reduce_fusion.1
  506.0 7.0 fusion.15
  513.0 6.5 copy.51
  519.5 5.2 all-to-all-start
  524.6 6.2 copy.53
  530.8 3.2 copy.80
  533.9 4.0 slice.55
  538.0 4.6 multiply_reduce_fusion
  542.6 7.0 multiply_convert_fusion
  549.6 6.2 maximum_bitcast_fusion
  555.8 9.1 pad_maximum_fusion
  564.9 15.1 %copy.55 = bf16[8,4,640,2,128]{4,2,3,1,0:T(8,128)(2,1)} copy(bf16[8,4,640,2,128]{2,4,3,1,0:T(8,128)(2,1)} %pad_maximum_fusion) | data formatting | bytes 20971520 | tf_op jit(solution)/shard_map/concatenate | solution.py:109
  580.0 38.3 %all-to-all-done = bf16[32,512,128]{2,1,0:T(8,128)(2,1)} async-done(((bf16[32,512,128]{2,1,0:T(8,128)(2,1)}), bf16[32,512,128]{2,1,0:T(8,128)(2,1)}, u32[]{:S(2)}, u32[]{:S(2)}) %all-to-all-start) | async-done | bytes 4194336 | tf_op jit(solution)/shard_map/all_to_all | solution.py:115
  618.3 6.0 all-to-all-start.1
  624.3 4.6 copy.52
  628.9 223.3 %all-to-all-done.1 = bf16[32,640,2,128]{3,1,2,0:T(8,128)(2,1)} async-done(((bf16[32,640,2,128]{3,1,2,0:T(8,128)(2,1)}), bf16[32,640,2,128]{3,1,2,0:T(8,128)(2,1)}, u32[]{:S(2)}, u32[]{:S(2)}) %all-to-all-start.1) | async-done | bytes 10485792 | tf_op jit(solution)/shard_map/all_to_all | solution.py:116
  852.2 9.2 copy.56
  861.4 118.3 %while.21 = (s32[]{:T(128)}, bf16[8,2048,128]{2,1,0:T(8,128)(2,1)}, bf16[8,2048,128]{2,1,0:T(8,128)(2,1)}, bf16[8,2560,2,128]{3,1,2,0:T(8,128)(2,1)}, s32[]{:T(128)}, /*index=5*/s32[]{:T(128)}, s32[]{:T(128)}) while((s32[]{:T(128)}, bf16[8,2048,128]{2,1,0:T(8,128)(2,1)}, bf16[8,2048,128]{2,1,0:T(8,128)(2,1)}, ...), condition=%wide.region_13.14_spmd, body=%wide.region_8.13_spmd.sunk | while | flops 680328192 | bytes 24652504 | solution.py:118
  861.4 1.4 dynamic-slice_bitcast_fusion.2
  864.0 11.4 %while.22 = (s32[]{:T(128)}, bf16[4,512,128]{2,1,0:T(8,128)(2,1)S(1)}, bf16[4,512,128]{2,1,0:T(8,128)(2,1)S(1)}, bf16[2560,128]{1,0:T(8,128)(2,1)S(1)}, bf16[2560,128]{1,0:T(8,128)(2,1)S(1)}, /*index=5*/s32[]{:T(128)}) while((s32[]{:T(128)}, bf16[4,512,128]{2,1,0:T(8,128)(2,1)S(1)}, bf16[4,512,128]{2,1,0:T(8,128)(2,1)S(1)}, ...), condition=%wide.region_12.12_spmd, body=%wide.region_9.11_spmd.sunk | while | flops 680328192 | bytes 17311820 | solution.py:47
  876.2 1.4 dynamic-slice_bitcast_fusion.2
  878.8 11.4 %while.22 = (s32[]{:T(128)}, bf16[4,512,128]{2,1,0:T(8,128)(2,1)S(1)}, bf16[4,512,128]{2,1,0:T(8,128)(2,1)S(1)}, bf16[2560,128]{1,0:T(8,128)(2,1)S(1)}, bf16[2560,128]{1,0:T(8,128)(2,1)S(1)}, /*index=5*/s32[]{:T(128)}) while((s32[]{:T(128)}, bf16[4,512,128]{2,1,0:T(8,128)(2,1)S(1)}, bf16[4,512,128]{2,1,0:T(8,128)(2,1)S(1)}, ...), condition=%wide.region_12.12_spmd, body=%wide.region_9.11_spmd.sunk | while | flops 680328192 | bytes 17311820 | solution.py:47
  891.0 1.4 dynamic-slice_bitcast_fusion.2
  893.6 11.3 %while.22 = (s32[]{:T(128)}, bf16[4,512,128]{2,1,0:T(8,128)(2,1)S(1)}, bf16[4,512,128]{2,1,0:T(8,128)(2,1)S(1)}, bf16[2560,128]{1,0:T(8,128)(2,1)S(1)}, bf16[2560,128]{1,0:T(8,128)(2,1)S(1)}, /*index=5*/s32[]{:T(128)}) while((s32[]{:T(128)}, bf16[4,512,128]{2,1,0:T(8,128)(2,1)S(1)}, bf16[4,512,128]{2,1,0:T(8,128)(2,1)S(1)}, ...), condition=%wide.region_12.12_spmd, body=%wide.region_9.11_spmd.sunk | while | flops 680328192 | bytes 17311820 | solution.py:47
  908.4 11.4 %while.22 = (s32[]{:T(128)}, bf16[4,512,128]{2,1,0:T(8,128)(2,1)S(1)}, bf16[4,512,128]{2,1,0:T(8,128)(2,1)S(1)}, bf16[2560,128]{1,0:T(8,128)(2,1)S(1)}, bf16[2560,128]{1,0:T(8,128)(2,1)S(1)}, /*index=5*/s32[]{:T(128)}) while((s32[]{:T(128)}, bf16[4,512,128]{2,1,0:T(8,128)(2,1)S(1)}, bf16[4,512,128]{2,1,0:T(8,128)(2,1)S(1)}, ...), condition=%wide.region_12.12_spmd, body=%wide.region_9.11_spmd.sunk | while | flops 680328192 | bytes 17311820 | solution.py:47
  920.6 1.4 dynamic-slice_bitcast_fusion.2
  923.2 11.4 %while.22 = (s32[]{:T(128)}, bf16[4,512,128]{2,1,0:T(8,128)(2,1)S(1)}, bf16[4,512,128]{2,1,0:T(8,128)(2,1)S(1)}, bf16[2560,128]{1,0:T(8,128)(2,1)S(1)}, bf16[2560,128]{1,0:T(8,128)(2,1)S(1)}, /*index=5*/s32[]{:T(128)}) while((s32[]{:T(128)}, bf16[4,512,128]{2,1,0:T(8,128)(2,1)S(1)}, bf16[4,512,128]{2,1,0:T(8,128)(2,1)S(1)}, ...), condition=%wide.region_12.12_spmd, body=%wide.region_9.11_spmd.sunk | while | flops 680328192 | bytes 17311820 | solution.py:47
  935.4 1.4 dynamic-slice_bitcast_fusion.2
  938.0 11.4 %while.22 = (s32[]{:T(128)}, bf16[4,512,128]{2,1,0:T(8,128)(2,1)S(1)}, bf16[4,512,128]{2,1,0:T(8,128)(2,1)S(1)}, bf16[2560,128]{1,0:T(8,128)(2,1)S(1)}, bf16[2560,128]{1,0:T(8,128)(2,1)S(1)}, /*index=5*/s32[]{:T(128)}) while((s32[]{:T(128)}, bf16[4,512,128]{2,1,0:T(8,128)(2,1)S(1)}, bf16[4,512,128]{2,1,0:T(8,128)(2,1)S(1)}, ...), condition=%wide.region_12.12_spmd, body=%wide.region_9.11_spmd.sunk | while | flops 680328192 | bytes 17311820 | solution.py:47
  952.7 11.4 %while.22 = (s32[]{:T(128)}, bf16[4,512,128]{2,1,0:T(8,128)(2,1)S(1)}, bf16[4,512,128]{2,1,0:T(8,128)(2,1)S(1)}, bf16[2560,128]{1,0:T(8,128)(2,1)S(1)}, bf16[2560,128]{1,0:T(8,128)(2,1)S(1)}, /*index=5*/s32[]{:T(128)}) while((s32[]{:T(128)}, bf16[4,512,128]{2,1,0:T(8,128)(2,1)S(1)}, bf16[4,512,128]{2,1,0:T(8,128)(2,1)S(1)}, ...), condition=%wide.region_12.12_spmd, body=%wide.region_9.11_spmd.sunk | while | flops 680328192 | bytes 17311820 | solution.py:47
  967.5 11.4 %while.22 = (s32[]{:T(128)}, bf16[4,512,128]{2,1,0:T(8,128)(2,1)S(1)}, bf16[4,512,128]{2,1,0:T(8,128)(2,1)S(1)}, bf16[2560,128]{1,0:T(8,128)(2,1)S(1)}, bf16[2560,128]{1,0:T(8,128)(2,1)S(1)}, /*index=5*/s32[]{:T(128)}) while((s32[]{:T(128)}, bf16[4,512,128]{2,1,0:T(8,128)(2,1)S(1)}, bf16[4,512,128]{2,1,0:T(8,128)(2,1)S(1)}, ...), condition=%wide.region_12.12_spmd, body=%wide.region_9.11_spmd.sunk | while | flops 680328192 | bytes 17311820 | solution.py:47
  979.7 4.9 copy.57
  984.6 95.2 %all_to_all.51 = bf16[8,2048,128]{2,0,1:T(8,128)(2,1)S(1)} all-to-all(bf16[8,2048,128]{2,0,1:T(8,128)(2,1)S(1)} %copy.57), channel_id=1, replica_groups=mesh['groups'=2,'seq'=4,'adapt'=4] {'seq'}, dimensions={1} | all-to-all | bytes 8388608 | tf_op jit(solution)/shard_map/all_to_all | solution.py:119
  1079.9 2.9 copy.59
  1082.8 6.6 copy.60
  1089.4 6.4 copy.61
  (159 shorter events, 113.8 us)
Async XLA Ops:
  6.5 5.0 copy-start
  6.5 123.1 %all-gather.6.cloned.1.call-start = ((), (), s32[]{:S(2)}) async-start(), calls=%async_computation.5 | async-start | bytes 7864320 | tf_op jit(solution)/shard_map/all_gather | solution.py:86
  11.5 239.9 %all-reduce.2.cloned.1.call-start = ((), (), s32[]{:S(2)}) async-start(), calls=%async_computation.4 | async-start | bytes 6291456 | tf_op jit(solution)/shard_map/psum | solution.py:85
  14.4 8.4 copy-start.2
  14.4 392.4 %all-gather.4.cloned.1.call-start = ((), (), s32[]{:S(2)}) async-start(), calls=%async_computation.3 | async-start | bytes 31457280 | tf_op jit(solution)/shard_map/all_gather | solution.py:90
  32.5 0.7 copy-start.4
  519.5 98.8 %all-to-all-start = ((bf16[32,512,128]{2,1,0:T(8,128)(2,1)}), bf16[32,512,128]{2,1,0:T(8,128)(2,1)}, u32[]{:S(2)}, u32[]{:S(2)}) async-start(bf16[32,512,128]{2,1,0:T(8,128)(2,1)} %bitcast.98), calls=%async_computation | async-start | bytes 8388608 | tf_op jit(solution)/shard_map/all_to_all | solution.py:115
  538.0 4.6 copy-start.3
  618.3 233.9 %all-to-all-start.1 = ((bf16[32,640,2,128]{3,1,2,0:T(8,128)(2,1)}), bf16[32,640,2,128]{3,1,2,0:T(8,128)(2,1)}, u32[]{:S(2)}, u32[]{:S(2)}) async-start(bf16[32,640,2,128]{3,1,2,0:T(8,128)(2,1)} %bitcast.96), calls=%async_computation.1 | async-start | bytes 20971520 | tf_op jit(solution)/shard_map/all_to_all | solution.py:116
  1082.8 13.0 %copy-start.1 = (bf16[4,3072,64]{1,2,0:T(8,128)(2,1)S(1)}, bf16[4,3072,64]{1,2,0:T(8,128)(2,1)}, u32[]{:S(2)}) copy-start(bf16[4,3072,64]{1,2,0:T(8,128)(2,1)} %param.17) | copy-start | bytes 4718596
Sparse Core Ops, SparseCore 0:
  11.6 118.0 all-gather.5
  132.0 119.2 all-reduce.1
  252.9 153.8 all-gather.3
